TPU v7x, 128 devices: a whole 4x4x4 slice. The times are simulated.
128 devices in a mesh: patch: 8 (over x, core), proto: 16 (over z, y).
Axes of the slice: x: 4, y: 4, z: 4, core: 2. Of those that a mesh axis runs over, the one named last changes fastest.
Arguments:
- student_feats: bfloat16 [32768, 256], P(('patch', 'proto')), may hold values from -50 to 50
- teacher_feats: bfloat16 [32768, 256], P(('patch', 'proto')), may hold values from -50 to 50
- proto_weight: bfloat16 [256, 131072], P(None, 'proto'), may hold values from -4 to 4
- mask_index: int32 [4096], P(('patch', 'proto')), may hold values from 0 to 255, as said below
- row_weight: bfloat16 [4096], P(('patch', 'proto')), may hold values from 0.5 to 4
Outputs:
- grad_student: float32 [4096, 256], P(('patch', 'proto'))
- grad_proto: float32 [256, 131072], P('patch', 'proto')
- loss: float32 [], replicated
Inputs may be any that keep to these rules, and one draw needn't show every extreme that they name: `mask_index`: entries k * 32 to (k + 1) * 32 - 1 are distinct patch positions of image k, counted from that image's first patch.
All inputs are finite; a program needn't handle non-finite values.
Results may differ from a plain program's by a relative error of at most 0.0057.
Values may be sent and summed in bfloat16 or wider, within the bound.
No kernel may reach another device: no remote copies, remote signals or barrier semaphores. Data moves between devices by JAX's collectives and lax.ppermute only.
A program may use at most 128 MiB of HBM per device.

v0:
```python
import jax
import jax.numpy as jnp
from jax import lax
from jax.sharding import PartitionSpec as P

SK_ITERS = 3
eps = 1e-06
teacher_temp = 0.07
student_temp = 0.1


def unit_rows(values):
    values = values.astype(jnp.float32)
    inverse = lax.rsqrt(jnp.sum(values * values, axis=1) + eps)
    return (values * inverse[:, None], inverse)


def finish(teacher_exp, scale_rows, scale_cols, logits, exp_logits, exp_total, weights):
    codes = teacher_exp * scale_rows[:, None] * scale_cols[None, :]
    student_probs = exp_logits / exp_total[:, None]
    grad_logits = (weights[:, None] * (student_probs - codes)).astype(jnp.bfloat16)
    log_total = jnp.log(exp_total)
    loss_partial = jnp.sum(weights[:, None] * codes * (log_total[:, None] - logits))
    return (grad_logits, loss_partial)


def feature_term(grad_logits, proto_cols):
    return (
        lax.dot_general(
            grad_logits, proto_cols, (((1,), (1,)), ((), ())), preferred_element_type=jnp.float32
        )
        / student_temp
    )


def head_term(student_rows, grad_logits):
    return (
        lax.dot_general(
            student_rows, grad_logits, (((0,), (0,)), ((), ())), preferred_element_type=jnp.float32
        )
        / student_temp
    )


def on_device(student_feats, teacher_feats, proto_weight, mask_index, row_weight):
    highest = lax.Precision.HIGHEST
    unit_student, inverse_student = unit_rows(jnp.take(student_feats, mask_index, axis=0))
    unit_teacher, _ = unit_rows(jnp.take(teacher_feats, mask_index, axis=0))
    own_student = unit_student.astype(jnp.bfloat16)
    own_teacher = unit_teacher.astype(jnp.bfloat16)
    w_float = proto_weight.astype(jnp.float32)
    col_inverse = lax.rsqrt(jnp.sum(w_float * w_float, axis=0) + eps)
    unit_proto = w_float * col_inverse[None, :]
    proto_unit = unit_proto.astype(jnp.bfloat16)
    teacher_rows, student_rows, weights = (
        lax.all_gather(own_teacher, "proto", axis=0, tiled=True),
        lax.all_gather(own_student, "proto", axis=0, tiled=True),
        lax.all_gather(row_weight, "proto", axis=0, tiled=True),
    )
    weights = weights.astype(jnp.float32)
    teacher_exp = jnp.exp(
        jnp.dot(teacher_rows, proto_unit, preferred_element_type=jnp.float32) / teacher_temp
    )
    scale_rows = jnp.ones((teacher_rows.shape[0],), jnp.float32)
    for sweep in range(SK_ITERS):
        col_part = jnp.dot(scale_rows, teacher_exp, precision=highest)
        scale_cols = 1.0 / lax.psum(col_part, "patch")
        row_part = jnp.dot(teacher_exp, scale_cols, precision=highest)
        scale_rows = 1.0 / lax.psum(row_part, "proto")
    logits = jnp.dot(student_rows, proto_unit, preferred_element_type=jnp.float32) / student_temp
    exp_logits = jnp.exp(logits)
    exp_total = lax.psum(jnp.sum(exp_logits, axis=1), "proto")
    grad_logits, loss_partial = finish(
        teacher_exp, scale_rows, scale_cols, logits, exp_logits, exp_total, weights
    )
    feature_grad = lax.psum_scatter(
        feature_term(grad_logits, proto_unit), "proto", scatter_dimension=0, tiled=True
    )
    row_share = proto_unit.shape[0] // lax.axis_size("patch")
    row_offset = lax.axis_index("patch") * row_share
    head_full = lax.psum(head_term(student_rows, grad_logits), "patch")
    inner = jnp.sum(unit_proto * head_full, axis=0)
    whole_grad = col_inverse[None, :] * (head_full - unit_proto * inner[None, :])
    grad_proto = lax.dynamic_slice_in_dim(whole_grad, row_offset, row_share, 0)
    loss_total, weight_total = lax.psum(
        (loss_partial, jnp.sum(row_weight.astype(jnp.float32))), ("patch", "proto")
    )
    grad_student = inverse_student[:, None] * (
        feature_grad - unit_student * jnp.sum(unit_student * feature_grad, axis=1)[:, None]
    )
    return (grad_student, grad_proto, loss_total / weight_total)


def solution(mesh):
    in_specs = (
        P(("patch", "proto"), None),
        P(("patch", "proto"), None),
        P(None, "proto"),
        P(("patch", "proto")),
        P(("patch", "proto")),
    )
    out_specs = (P(("patch", "proto"), None), P("patch", "proto"), P())
    return jax.shard_map(
        on_device, mesh=mesh, in_specs=in_specs, out_specs=out_specs, check_vma=False
    )
```

profile of v0, /device:TPU:1, one launch (start us, length us, event | category | flops | bytes accessed | tf_op | source)
XLA Modules:
  0.0 526.8 jit_solution(3142531026962949100)
XLA Ops:
  11.9 20.8 %all_gather.11 = bf16[512,256]{1,0:T(8,128)(2,1)S(1)} all-gather(bf16[32,256]{1,0:T(8,128)(2,1)S(1)} %get-tuple-element.15), channel_id=1, replica_groups=mesh['patch'=8,'proto'=16] {'proto'}, dimensions={0}, use_global_device_ids=true | all-gather | bytes 278528 | tf_op jit(solution)/shard_map/all_gather | solution.py:56
  35.8 4.5 multiply_exponential_fusion
  40.3 7.9 %fusion.20 = f32[1,8192]{1,0:T(1,128)S(1)} fusion(f32[512,8192]{1,0:T(8,128)S(1)} %multiply_exponential_fusion), kind=kOutput, calls=%fused_computation.41 | convolution fusion | flops 50331648 | bytes 16809984 | tf_op jit(solution)/shard_map/dot_general | solution.py:66
  48.2 26.1 %psum.71 = f32[8192]{0:T(1024)S(1)} all-reduce(f32[8192]{0:T(1024)S(1)} %bitcast.33), channel_id=1, replica_groups=mesh['patch'=8,'proto'=16] {'patch'}, use_global_device_ids=true, to_apply=%region_5.7 | all-reduce | flops 8192 | bytes 65536 | tf_op jit(solution)/shard_map/psum | solution.py:67
  74.4 17.6 %fusion.23 = f32[1,512]{1,0:T(1,128)S(1)} fusion(f32[512,8192]{1,0:T(8,128)} %copy-done.2, f32[8192,1]{0,1:T(1,128)S(1)} %bitcast.29), kind=kOutput, calls=%fused_computation.50 | convolution fusion | flops 50331648 | bytes 16812032 | tf_op jit(solution)/shard_map/dot_general | solution.py:68
  92.0 31.0 %psum.72 = f32[512]{0:T(512)S(1)} all-reduce(f32[512]{0:T(512)S(1)} %bitcast.35), channel_id=1, replica_groups=mesh['patch'=8,'proto'=16] {'proto'}, use_global_device_ids=true, to_apply=%region_6.8 | all-reduce | flops 512 | bytes 4096 | tf_op jit(solution)/shard_map/psum | solution.py:69
  123.0 11.5 %fusion.24 = f32[1,8192]{1,0:T(1,128)S(1)} fusion(f32[512,1]{0,1:T(1,128)S(1)} %bitcast.37, f32[512,8192]{1,0:T(8,128)} %copy-done.2), kind=kOutput, calls=%fused_computation.51 | convolution fusion | flops 50331648 | bytes 16812032 | tf_op jit(solution)/shard_map/dot_general | solution.py:66
  134.5 30.9 %psum.73 = f32[8192]{0:T(1024)S(1)} all-reduce(f32[8192]{0:T(1024)S(1)} %bitcast.30), channel_id=1, replica_groups=mesh['patch'=8,'proto'=16] {'patch'}, use_global_device_ids=true, to_apply=%region_7.9 | all-reduce | flops 8192 | bytes 65536 | tf_op jit(solution)/shard_map/psum | solution.py:67
  165.4 17.6 %fusion.25 = f32[1,512]{1,0:T(1,128)S(1)} fusion(f32[512,8192]{1,0:T(8,128)} %copy-done.2, f32[8192,1]{0,1:T(1,128)S(1)} %bitcast.31), kind=kOutput, calls=%fused_computation.52 | convolution fusion | flops 50331648 | bytes 16812032 | tf_op jit(solution)/shard_map/dot_general | solution.py:68
  183.0 28.5 %psum.74 = f32[512]{0:T(512)S(1)} all-reduce(f32[512]{0:T(512)S(1)} %bitcast.36), channel_id=1, replica_groups=mesh['patch'=8,'proto'=16] {'proto'}, use_global_device_ids=true, to_apply=%region_8.10 | all-reduce | flops 512 | bytes 4096 | tf_op jit(solution)/shard_map/psum | solution.py:69
  211.5 11.5 %fusion.26 = f32[1,8192]{1,0:T(1,128)S(1)} fusion(f32[512,1]{0,1:T(1,128)S(1)} %bitcast.38, f32[512,8192]{1,0:T(8,128)} %copy-done.2), kind=kOutput, calls=%fused_computation.53 | convolution fusion | flops 50331648 | bytes 16812032 | tf_op jit(solution)/shard_map/dot_general | solution.py:66
  223.0 31.0 %psum.75 = f32[8192]{0:T(1024)S(1)} all-reduce(f32[8192]{0:T(1024)S(1)} %bitcast.32), channel_id=1, replica_groups=mesh['patch'=8,'proto'=16] {'patch'}, use_global_device_ids=true, to_apply=%region_9.11 | all-reduce | flops 8192 | bytes 65536 | tf_op jit(solution)/shard_map/psum | solution.py:67
  254.0 17.8 %fusion.27 = f32[1,512]{1,0:T(1,128)S(1)} fusion(f32[512,8192]{1,0:T(8,128)} %copy-done.2, f32[8192,1]{0,1:T(1,128)S(1)} %bitcast.28), kind=kOutput, calls=%fused_computation.54 | convolution fusion | flops 50331648 | bytes 16812032 | tf_op jit(solution)/shard_map/dot_general | solution.py:68
  271.7 17.8 %all_gather.10 = bf16[512,256]{1,0:T(8,128)(2,1)S(1)} all-gather(bf16[32,256]{1,0:T(8,128)(2,1)S(1)} %get-tuple-element.14), channel_id=1, replica_groups=mesh['patch'=8,'proto'=16] {'proto'}, dimensions={0}, use_global_device_ids=true | all-gather | bytes 278528 | tf_op jit(solution)/shard_map/all_gather | solution.py:57
  289.5 7.5 %exponential_reduce_fusion = (f32[512]{0:T(512)S(1)}, f32[512,8192]{1,0:T(8,128)}) fusion(bf16[512,256]{1,0:T(8,128)(2,1)S(1)} %all_gather.10, f32[8192]{0:T(1024)S(1)} %add_rsqrt_fusion, bf16[256,8192]{1,0:T(8,128)(2,1)S(1)} %copy-done.3), kind=kOutput, calls=%fused_computation.6 | convolution fusion | flops 2162163200 | bytes 21268480 | tf_op jit(solution)/shard_map/dot_general | solution.py:70
  297.0 30.9 %all-reduce.2 = (f32[512]{0:T(512)S(1)}, f32[512]{0:T(512)S(1)}) all-reduce(f32[512]{0:T(512)S(1)} %bitcast.34, f32[512]{0:T(512)S(1)} %get-tuple-element.16), channel_id=1, replica_groups=mesh['patch'=8,'proto'=16] {'proto'}, use_global_device_ids=true, to_apply=%region_10.12 | all-reduce | flops 1024 | bytes 8192 | tf_op jit(solution)/shard_map/psum | solution.py:69
  329.4 29.0 %all-reduce = bf16[512]{0:T(512)(128)(2,1)S(1)} all-reduce(bf16[512]{0:T(512)(128)(2,1)S(1)} %dynamic-update-slice), channel_id=1, replica_groups=mesh['patch'=8,'proto'=16] {'proto'}, use_global_device_ids=true, to_apply=%add | all-reduce | flops 512 | bytes 2048
  358.4 14.4 %multiply_reduce_fusion = (f32[]{:T(128)}, bf16[512,8192]{1,0:T(8,128)(2,1)S(1)}) fusion(f32[512,8192]{1,0:T(8,128)} %copy-done.2, f32[512,8192]{1,0:T(8,128)} %get-tuple-element.17, f32[512]{0:T(512)S(1)} %log.3, f32[8192]{0:T(1024)S(1)} %broadcast_divide_fusion, f32[512]{0:T(512)S(1)} %broadcast_divide_fusion.5, f32[512]{0:T(512)S(1)} %convert_element_type.28, ...), kind=kLoop, calls=%fused_computation.2 | loop fusion | flops 46137344 | bytes 41984004 | tf_op jit(solution)/shard_map/reduce_sum | solution.py:23
  372.9 3.2 copy-done.5
  376.1 3.2 fusion.7
  379.4 9.0 %convolution_multiply_fusion = f32[256,8192]{1,0:T(8,128)} fusion(bf16[512,256]{1,0:T(8,128)(2,1)S(1)} %all_gather.10, bf16[512,8192]{1,0:T(8,128)(2,1)} %copy-done.5), kind=kOutput, calls=%fused_computation.7 | convolution fusion | flops 2149580800 | bytes 17039360 | tf_op jit(solution)/shard_map/dot_general | solution.py:38
  389.0 85.0 %all-reduce.1 = (f32[]{:T(128)}, f32[]{:T(128)}) all-reduce(f32[]{:T(128)} %get-tuple-element.10, f32[]{:T(128)} %convert_reduce_fusion), channel_id=1, replica_groups=mesh['patch'=8,'proto'=16] {'patch','proto'}, use_global_device_ids=true, to_apply=%region_16.18 | all-reduce | flops 2 | bytes 16 | tf_op jit(solution)/shard_map/psum | solution.py:85
  477.8 32.0 %all-reduce.5.cloned.1.call-done = f32[256,8192]{1,0:T(8,128)} async-done(((f32[256,8192]{1,0:T(8,128)}), f32[256,8192]{1,0:T(8,128)}) %all-reduce.5.cloned.1.call-update) | async-done | bytes 8388624 | tf_op jit(solution)/shard_map/psum | solution.py:81
  509.8 6.0 %multiply_reduce_fusion.1 = (f32[8192]{0:T(1024)S(1)}, f32[256,8192]{1,0:T(8,128)S(1)}) fusion(f32[256,8192]{1,0:T(8,128)} %all-reduce.5.cloned.1.call-done, f32[8192]{0:T(1024)S(1)} %add_rsqrt_fusion, bf16[256,8192]{1,0:T(8,128)(2,1)} %param.9), kind=kLoop, calls=%fused_computation.11 | loop fusion | flops 8380416 | bytes 21037056 | tf_op jit(solution)/shard_map/reduce_sum | solution.py:82
  (45 shorter events, 13.3 us)
Async XLA Ops:
  8.0 1.4 copy-start
  8.0 467.3 %reduce-scatter.2.cloned.1.call-start = ((), (), s32[]{:S(2)}) async-start(), calls=%async_computation.1 | async-start | bytes 557056 | tf_op jit(solution)/shard_map/reduce_scatter | solution.py:76
  40.3 8.0 %copy-start.2 = (f32[512,8192]{1,0:T(8,128)}, f32[512,8192]{1,0:T(8,128)S(1)}, u32[]{:S(2)}) copy-start(f32[512,8192]{1,0:T(8,128)S(1)} %multiply_exponential_fusion) | copy-start | bytes 50331652
  253.9 35.6 %copy-start.3 = (bf16[256,8192]{1,0:T(8,128)(2,1)S(1)}, bf16[256,8192]{1,0:T(8,128)(2,1)}, u32[]{:S(2)}) copy-start(bf16[256,8192]{1,0:T(8,128)(2,1)} %param.9) | copy-start | bytes 12582916
  289.5 38.4 %copy-start.7 = (u32[128]{0:T(128)S(1)}, u32[128]{0:T(128)}, u32[]{:S(2)}) copy-start(u32[128]{0:T(128)} %constant.44) | copy-start | bytes 1540
  289.5 39.6 %copy-start.6 = (bf16[32]{0:T(256)(128)(2,1)S(1)}, bf16[32]{0:T(256)(128)(2,1)}, u32[]{:S(2)}) copy-start(bf16[32]{0:T(256)(128)(2,1)} %param.11) | copy-start | bytes 196
  358.4 17.7 %copy-start.4 = (bf16[256,8192]{1,0:T(8,128)(2,1)S(1)}, bf16[256,8192]{1,0:T(8,128)(2,1)}, u32[]{:S(2)}) copy-start(bf16[256,8192]{1,0:T(8,128)(2,1)} %param.9) | copy-start | bytes 12582916
  372.9 3.2 copy-start.5
  379.3 130.5 %all-reduce.5.cloned.1.call-start = ((), (), s32[]{:S(2)}) async-start(), calls=%async_computation.2 | async-start | bytes 16777216 | tf_op jit(solution)/shard_map/psum | solution.py:81
  476.2 41.8 %copy-start.1 = (bf16[256,256]{1,0:T(8,128)(2,1)S(1)}, bf16[256,256]{1,0:T(8,128)(2,1)}, u32[]{:S(2)}) copy-start(bf16[256,256]{1,0:T(8,128)(2,1)} %param.7) | copy-start | bytes 393220
Sparse Core Ops, SparseCore 0:
  379.4 87.7 reduce-scatter.1
Sparse Core Ops, SparseCore 1:
  388.5 121.3 all-reduce.4
where the time goes:
time: 536 us; the launch traced here: 527 us
  blocking collectives  331 us (62%)
  matrix products  108 us (20%)
  waiting for transfers between devices  32.1 us (6%)
  other arithmetic  30.5 us (6%)
  between operations  18.9 us (4%)
  local copies, waits for them, and re-layouts  6.24 us (1%)
    psum x3, blocking collectives, on_device(): scale_rows = 1.0 / lax.psum(row_part, 'proto')  90.4 us
    psum x3, blocking collectives, on_device(): scale_cols = 1.0 / lax.psum(col_part, 'patch')  88 us
    psum x1, blocking collectives, on_device(): lax.psum((loss_partial, jnp.sum(row_weight.astype(jnp.float32))), ('patch...  85 us
    dot_general x3, matrix products, on_device(): row_part = jnp.dot(teacher_exp, scale_cols, precision=highest)  53 us
    psum x1, waiting for transfers between devices, on_device(): head_full = lax.psum(head_term(student_rows, grad_logits), 'patch')  32 us
    dot_general x3, matrix products, on_device(): col_part = jnp.dot(scale_rows, teacher_exp, precision=highest)  30.8 us
    unnamed x1, blocking collectives  29 us
    all_gather x1, blocking collectives, on_device(): lax.all_gather(own_teacher, 'proto', axis=0, tiled=True)  20.8 us
  transfers between devices with their start and end apart: 2, of which 1 were waited for; matrix products, arithmetic and copies ran while one was open for 2% of the time, Pallas kernels for 0%

commit v1 on v0

--- a/solution.py
+++ b/solution.py
@@ -78,7 +78,7 @@
     )
     row_share = proto_unit.shape[0] // lax.axis_size("patch")
     row_offset = lax.axis_index("patch") * row_share
-    head_full = lax.psum(head_term(student_rows, grad_logits), "patch")
+    head_full = jnp.sum(lax.all_gather(head_term(student_rows, grad_logits), "patch"), axis=0)
     inner = jnp.sum(unit_proto * head_full, axis=0)
     whole_grad = col_inverse[None, :] * (head_full - unit_proto * inner[None, :])
     grad_proto = lax.dynamic_slice_in_dim(whole_grad, row_offset, row_share, 0)

time: 536 us -> 756 us (1.41)
  waiting for transfers between devices: 32.1 us -> 226 us
  other arithmetic: 30.5 us -> 54.9 us
    all_gather x0 -> x1, waiting for transfers between devices: none -> 226 us  [on_device(): lax.all_gather(head_term(student_rows, grad_logits), 'patch')]
    psum x1 -> x0, waiting for transfers between devices: 32 us -> none  [on_device(): head_full = lax.psum(head_term(student_rows, grad_logits), 'patch')]
    reduce_sum x0 -> x1, other arithmetic: none -> 24.4 us  [on_device(): jnp.sum(lax.all_gather(head_term(student_rows, grad_logits), 'patch'), ax...]
where the time goes in v1:
time: 756 us; the launch traced here: 746 us
  blocking collectives  331 us (44%)
  waiting for transfers between devices  226 us (30%)
  matrix products  108 us (14%)
  other arithmetic  54.9 us (7%)
  between operations  18.9 us (2%)
    all_gather x1, waiting for transfers between devices, on_device(): lax.all_gather(head_term(student_rows, grad_logits), 'patch')  226 us
    psum x3, blocking collectives, on_device(): scale_cols = 1.0 / lax.psum(col_part, 'patch')  93.9 us
    psum x3, blocking collectives, on_device(): scale_rows = 1.0 / lax.psum(row_part, 'proto')  89.9 us
    psum x1, blocking collectives, on_device(): lax.psum((loss_partial, jnp.sum(row_weight.astype(jnp.float32))), ('patch...  80.2 us
    dot_general x3, matrix products, on_device(): row_part = jnp.dot(teacher_exp, scale_cols, precision=highest)  52.8 us
    dot_general x3, matrix products, on_device(): col_part = jnp.dot(scale_rows, teacher_exp, precision=highest)  30.8 us
    unnamed x1, blocking collectives  28.7 us
    reduce_sum x1, other arithmetic, on_device(): jnp.sum(lax.all_gather(head_term(student_rows, grad_logits), 'patch'), ax...  24.4 us
  transfers between devices with their start and end apart: 2, of which 1 were waited for; matrix products, arithmetic and copies ran while one was open for 2% of the time, Pallas kernels for 0%

profile of v1, /device:TPU:1, one launch (start us, length us, event | category | flops | bytes accessed | tf_op | source)
XLA Modules:
  0.0 745.6 jit_solution(15844610642327376719)
XLA Ops:
  11.9 21.1 %all_gather.17 = bf16[512,256]{1,0:T(8,128)(2,1)S(1)} all-gather(bf16[32,256]{1,0:T(8,128)(2,1)S(1)} %get-tuple-element.15), channel_id=1, replica_groups=mesh['patch'=8,'proto'=16] {'proto'}, dimensions={0}, use_global_device_ids=true | all-gather | bytes 278528 | tf_op jit(solution)/shard_map/all_gather | solution.py:56
  36.1 17.4 %all_gather.16 = bf16[512,256]{1,0:T(8,128)(2,1)S(1)} all-gather(bf16[32,256]{1,0:T(8,128)(2,1)S(1)} %get-tuple-element.14), channel_id=1, replica_groups=mesh['patch'=8,'proto'=16] {'proto'}, dimensions={0}, use_global_device_ids=true | all-gather | bytes 278528 | tf_op jit(solution)/shard_map/all_gather | solution.py:57
  53.5 4.5 multiply_exponential_fusion
  58.0 8.0 %exponential_reduce_fusion = (f32[512]{0:T(512)S(1)}, f32[512,8192]{1,0:T(8,128)}) fusion(bf16[512,256]{1,0:T(8,128)(2,1)S(1)} %all_gather.16, f32[8192]{0:T(1024)S(1)} %add_rsqrt_fusion, bf16[256,8192]{1,0:T(8,128)(2,1)S(1)} %copy-done.3), kind=kOutput, calls=%fused_computation.6 | convolution fusion | flops 2162163200 | bytes 21268480 | tf_op jit(solution)/shard_map/dot_general | solution.py:70
  65.9 7.9 %fusion.20 = f32[1,8192]{1,0:T(1,128)S(1)} fusion(f32[512,8192]{1,0:T(8,128)S(1)} %multiply_exponential_fusion), kind=kOutput, calls=%fused_computation.41 | convolution fusion | flops 50331648 | bytes 16809984 | tf_op jit(solution)/shard_map/dot_general | solution.py:66
  73.9 31.9 %psum.64 = f32[8192]{0:T(1024)S(1)} all-reduce(f32[8192]{0:T(1024)S(1)} %bitcast.34), channel_id=1, replica_groups=mesh['patch'=8,'proto'=16] {'patch'}, use_global_device_ids=true, to_apply=%region_5.7 | all-reduce | flops 8192 | bytes 65536 | tf_op jit(solution)/shard_map/psum | solution.py:67
  105.8 17.6 %fusion.23 = f32[1,512]{1,0:T(1,128)S(1)} fusion(f32[512,8192]{1,0:T(8,128)} %copy-done.2, f32[8192,1]{0,1:T(1,128)S(1)} %bitcast.30), kind=kOutput, calls=%fused_computation.50 | convolution fusion | flops 50331648 | bytes 16812032 | tf_op jit(solution)/shard_map/dot_general | solution.py:68
  123.4 31.0 %psum.65 = f32[512]{0:T(512)S(1)} all-reduce(f32[512]{0:T(512)S(1)} %bitcast.36), channel_id=1, replica_groups=mesh['patch'=8,'proto'=16] {'proto'}, use_global_device_ids=true, to_apply=%region_6.8 | all-reduce | flops 512 | bytes 4096 | tf_op jit(solution)/shard_map/psum | solution.py:69
  154.4 11.5 %fusion.24 = f32[1,8192]{1,0:T(1,128)S(1)} fusion(f32[512,1]{0,1:T(1,128)S(1)} %bitcast.38, f32[512,8192]{1,0:T(8,128)} %copy-done.2), kind=kOutput, calls=%fused_computation.51 | convolution fusion | flops 50331648 | bytes 16812032 | tf_op jit(solution)/shard_map/dot_general | solution.py:66
  165.9 30.9 %psum.66 = f32[8192]{0:T(1024)S(1)} all-reduce(f32[8192]{0:T(1024)S(1)} %bitcast.31), channel_id=1, replica_groups=mesh['patch'=8,'proto'=16] {'patch'}, use_global_device_ids=true, to_apply=%region_7.9 | all-reduce | flops 8192 | bytes 65536 | tf_op jit(solution)/shard_map/psum | solution.py:67
  196.8 17.6 %fusion.25 = f32[1,512]{1,0:T(1,128)S(1)} fusion(f32[512,8192]{1,0:T(8,128)} %copy-done.2, f32[8192,1]{0,1:T(1,128)S(1)} %bitcast.32), kind=kOutput, calls=%fused_computation.52 | convolution fusion | flops 50331648 | bytes 16812032 | tf_op jit(solution)/shard_map/dot_general | solution.py:68
  214.4 28.5 %psum.67 = f32[512]{0:T(512)S(1)} all-reduce(f32[512]{0:T(512)S(1)} %bitcast.37), channel_id=1, replica_groups=mesh['patch'=8,'proto'=16] {'proto'}, use_global_device_ids=true, to_apply=%region_8.10 | all-reduce | flops 512 | bytes 4096 | tf_op jit(solution)/shard_map/psum | solution.py:69
  242.9 11.5 %fusion.26 = f32[1,8192]{1,0:T(1,128)S(1)} fusion(f32[512,1]{0,1:T(1,128)S(1)} %bitcast.39, f32[512,8192]{1,0:T(8,128)} %copy-done.2), kind=kOutput, calls=%fused_computation.53 | convolution fusion | flops 50331648 | bytes 16812032 | tf_op jit(solution)/shard_map/dot_general | solution.py:66
  254.4 31.1 %psum.68 = f32[8192]{0:T(1024)S(1)} all-reduce(f32[8192]{0:T(1024)S(1)} %bitcast.33), channel_id=1, replica_groups=mesh['patch'=8,'proto'=16] {'patch'}, use_global_device_ids=true, to_apply=%region_9.11 | all-reduce | flops 8192 | bytes 65536 | tf_op jit(solution)/shard_map/psum | solution.py:67
  285.5 17.6 %fusion.27 = f32[1,512]{1,0:T(1,128)S(1)} fusion(f32[512,8192]{1,0:T(8,128)} %copy-done.2, f32[8192,1]{0,1:T(1,128)S(1)} %bitcast.29), kind=kOutput, calls=%fused_computation.54 | convolution fusion | flops 50331648 | bytes 16812032 | tf_op jit(solution)/shard_map/dot_general | solution.py:68
  303.1 30.4 %all-reduce.2 = (f32[512]{0:T(512)S(1)}, f32[512]{0:T(512)S(1)}) all-reduce(f32[512]{0:T(512)S(1)} %bitcast.35, f32[512]{0:T(512)S(1)} %get-tuple-element.16), channel_id=1, replica_groups=mesh['patch'=8,'proto'=16] {'proto'}, use_global_device_ids=true, to_apply=%region_10.12 | all-reduce | flops 1024 | bytes 8192 | tf_op jit(solution)/shard_map/psum | solution.py:69
  335.0 28.7 %all-reduce = bf16[512]{0:T(512)(128)(2,1)S(1)} all-reduce(bf16[512]{0:T(512)(128)(2,1)S(1)} %dynamic-update-slice), channel_id=1, replica_groups=mesh['patch'=8,'proto'=16] {'proto'}, use_global_device_ids=true, to_apply=%add | all-reduce | flops 512 | bytes 2048
  363.7 14.4 %multiply_reduce_fusion = (f32[]{:T(128)}, bf16[512,8192]{1,0:T(8,128)(2,1)S(1)}) fusion(f32[512,8192]{1,0:T(8,128)} %copy-done.2, f32[512,8192]{1,0:T(8,128)} %get-tuple-element.17, f32[512]{0:T(512)S(1)} %log.3, f32[8192]{0:T(1024)S(1)} %broadcast_divide_fusion, f32[512]{0:T(512)S(1)} %broadcast_divide_fusion.5, f32[512]{0:T(512)S(1)} %convert_element_type.28, ...), kind=kLoop, calls=%fused_computation.2 | loop fusion | flops 46137344 | bytes 41984004 | tf_op jit(solution)/shard_map/reduce_sum | solution.py:23
  378.2 3.2 copy-done.5
  384.8 8.9 %convolution_multiply_fusion = f32[256,8192]{1,0:T(8,128)} fusion(bf16[512,256]{1,0:T(8,128)(2,1)S(1)} %all_gather.16, bf16[512,8192]{1,0:T(8,128)(2,1)} %copy-done.5), kind=kOutput, calls=%fused_computation.7 | convolution fusion | flops 2149580800 | bytes 17039360 | tf_op jit(solution)/shard_map/dot_general | solution.py:38
  394.4 80.2 %all-reduce.1 = (f32[]{:T(128)}, f32[]{:T(128)}) all-reduce(f32[]{:T(128)} %get-tuple-element.10, f32[]{:T(128)} %convert_reduce_fusion), channel_id=1, replica_groups=mesh['patch'=8,'proto'=16] {'patch','proto'}, use_global_device_ids=true, to_apply=%region_16.18 | all-reduce | flops 2 | bytes 16 | tf_op jit(solution)/shard_map/psum | solution.py:85
  478.4 225.8 %all-gather.3.cloned.1.call-done = f32[2048,8192]{1,0:T(8,128)} async-done(((f32[256,8192]{1,0:T(8,128)}), f32[2048,8192]{1,0:T(8,128)}) %all-gather.3.cloned.1.call-update) | async-done | bytes 67108880 | tf_op jit(solution)/shard_map/all_gather | solution.py:81
  704.2 24.4 %reduce_sum.86 = f32[256,8192]{1,0:T(8,128)} reduce(f32[8,256,8192]{2,1,0:T(8,128)} %bitcast.12, f32[]{:T(128)} %constant.18.clone.1), dimensions={0}, to_apply=%region_13.15 | reduce | flops 14680064 | bytes 75497472 | tf_op jit(solution)/shard_map/reduce_sum | solution.py:81
  728.6 6.0 multiply_reduce_fusion.1
  (46 shorter events, 16.6 us)
Async XLA Ops:
  8.0 1.4 copy-start
  8.0 467.9 %reduce-scatter.2.cloned.1.call-start = ((), (), s32[]{:S(2)}) async-start(), calls=%async_computation.1 | async-start | bytes 557056 | tf_op jit(solution)/shard_map/reduce_scatter | solution.py:76
  11.6 46.4 %copy-start.3 = (bf16[256,8192]{1,0:T(8,128)(2,1)S(1)}, bf16[256,8192]{1,0:T(8,128)(2,1)}, u32[]{:S(2)}) copy-start(bf16[256,8192]{1,0:T(8,128)(2,1)} %param.9) | copy-start | bytes 12582916
  58.0 15.9 %copy-start.2 = (f32[512,8192]{1,0:T(8,128)}, f32[512,8192]{1,0:T(8,128)S(1)}, u32[]{:S(2)}) copy-start(f32[512,8192]{1,0:T(8,128)S(1)} %multiply_exponential_fusion) | copy-start | bytes 50331652
  254.4 79.1 %copy-start.7 = (u32[128]{0:T(128)S(1)}, u32[128]{0:T(128)}, u32[]{:S(2)}) copy-start(u32[128]{0:T(128)} %constant.44) | copy-start | bytes 1540
  254.4 80.4 %copy-start.6 = (bf16[32]{0:T(256)(128)(2,1)S(1)}, bf16[32]{0:T(256)(128)(2,1)}, u32[]{:S(2)}) copy-start(bf16[32]{0:T(256)(128)(2,1)} %param.11) | copy-start | bytes 196
  363.7 17.7 %copy-start.4 = (bf16[256,8192]{1,0:T(8,128)(2,1)S(1)}, bf16[256,8192]{1,0:T(8,128)(2,1)}, u32[]{:S(2)}) copy-start(bf16[256,8192]{1,0:T(8,128)(2,1)} %param.9) | copy-start | bytes 12582916
  378.1 3.2 copy-start.5
  384.6 319.6 %all-gather.3.cloned.1.call-start = ((), (), s32[]{:S(2)}) async-start(), calls=%async_computation.2 | async-start | bytes 75497472 | tf_op jit(solution)/shard_map/all_gather | solution.py:81
  704.2 32.7 %copy-start.1 = (bf16[256,256]{1,0:T(8,128)(2,1)S(1)}, bf16[256,256]{1,0:T(8,128)(2,1)}, u32[]{:S(2)}) copy-start(bf16[256,256]{1,0:T(8,128)(2,1)} %param.7) | copy-start | bytes 393220
Sparse Core Ops, SparseCore 0:
  384.7 83.1 reduce-scatter.1
Sparse Core Ops, SparseCore 1:
  393.9 310.3 all-gather.2
